TPU v7x, 32 devices: a whole 2x2x4 slice. The times are simulated.
32 devices in a mesh: wide: 8 (over y, x, core), narrow: 4 (over z).
Axes of the slice: x: 2, y: 2, z: 4, core: 2. Of those that a mesh axis runs over, the one named last changes fastest.
Arguments:
- tokens: float32 [4488, 768], P('wide'), may hold values from -6 to 6
- region: int32 [4488], P('wide'), may hold values from 0 to 59, as said below
- order_rank: int32 [4488], P('wide'), may hold values from 0 to 559, as said below
- box_coords: int32 [2, 4488], P(None, 'wide'), may hold values from 0 to 127
- w_query: float32 [768, 768], P(None, 'narrow'), may hold values from -0.21875 to 0.21875
- b_query: float32 [768], P('narrow'), may hold values from -3 to 3
- w_key: float32 [768, 768], P(None, 'narrow'), may hold values from -0.21875 to 0.21875
- w_value: float32 [768, 768], P(None, 'narrow'), may hold values from -0.21875 to 0.21875
- b_value: float32 [768], P('narrow'), may hold values from -0.18 to 0.18
- w_out: float32 [768, 768], P('narrow'), may hold values from -2 to 2
- b_out: float32 [768], replicated, may hold values from -2 to 2
- ln1_gain: float32 [768], replicated, may hold values from 0.1 to 1.9
- ln1_bias: float32 [768], replicated, may hold values from -2 to 2
- w_in: float32 [768, 3072], P(None, 'narrow'), may hold values from -0.21875 to 0.21875
- b_in: float32 [3072], P('narrow'), may hold values from -2 to 2
- w_down: float32 [3072, 768], P('narrow'), may hold values from -0.109375 to 0.109375
- b_down: float32 [768], replicated, may hold values from -2 to 2
- ln2_gain: float32 [768], replicated, may hold values from 0.1 to 1.9
- ln2_bias: float32 [768], replicated, may hold values from -2 to 2
- rel_order: float32 [12, 32], P('narrow'), may hold values from -3 to 3
- rel_x: float32 [12, 64], P('narrow'), may hold values from -3 to 3
- rel_y: float32 [12, 64], P('narrow'), may hold values from -3 to 3
- cotangent: float32 [4488, 768], P('wide'), may hold values from -6 to 6
Outputs:
- output: float32 [4488, 768], P('wide')
- grad_input: float32 [4488, 768], P('wide')
- grad_w_query: float32 [768, 768], P(None, 'narrow')
- grad_b_query: float32 [768], P('narrow')
- grad_w_key: float32 [768, 768], P(None, 'narrow')
- grad_w_value: float32 [768, 768], P(None, 'narrow')
- grad_b_value: float32 [768], P('narrow')
- grad_w_out: float32 [768, 768], P('narrow')
- grad_b_out: float32 [768], replicated
- grad_ln1_gain: float32 [768], replicated
- grad_ln1_bias: float32 [768], replicated
- grad_w_in: float32 [768, 3072], P(None, 'narrow')
- grad_b_in: float32 [3072], P('narrow')
- grad_w_down: float32 [3072, 768], P('narrow')
- grad_b_down: float32 [768], replicated
- grad_ln2_gain: float32 [768], replicated
- grad_ln2_bias: float32 [768], replicated
- grad_rel_order: float32 [12, 32], P('narrow')
- grad_rel_x: float32 [12, 64], P('narrow')
- grad_rel_y: float32 [12, 64], P('narrow')
Inputs may be any that keep to these rules, and one draw needn't show every extreme that they name: Each page's region ids take every value from 0 to its region count minus 1; region counts run from 2 to min(60, 561), and one page has the most. `order_rank`: within each region of a page the ranks are 0, 1, and so on up to its size minus 1, each once; no region holds more than 560 tokens, and one page has a region of exactly 560 tokens.
All inputs are finite; a program needn't handle non-finite values.
Results may differ from a plain program's by a relative error of at most 0.015.
The roundings to bfloat16 on the way count: a program that leaves them out, or rounds other values in their place, can miss the bound.
Values sent between devices are 32-bit elements; how exact they have to be, the bound alone decides.
A program may use at most 128 MiB of HBM per device.

v0:
```python
import math
import jax
import jax.numpy as jnp
from jax import lax
from jax.sharding import PartitionSpec as P

HEAD_DIM = 64
BINS1 = 32
BINS2 = 64
MAX_ORDER = 128
MAX_LAYOUT = 256
PAGE = 561
HIGHEST = lax.Precision.HIGHEST
EPSILON = 1e-05
SCORE_SCALE = 0.125


def bucket_steps(bins, reach):
    halfway = bins // 2
    exact = halfway // 2
    steps = []
    for level in range(1, halfway):
        if level < exact:
            steps.append(level)
        else:
            found = reach + 1
            for count in range(exact, reach + 2):
                value = exact + int(
                    math.log(count / exact) / math.log(reach / exact) * (halfway - exact)
                )
                if min(value, halfway - 1) >= level:
                    found = count
                    break
            steps.append(found)
    return steps


def bucket_of(offset_grid, bins, reach):
    halfway = bins // 2
    magnitude = jnp.abs(offset_grid)
    result = jnp.where(offset_grid > 0, halfway, 0).astype(jnp.int32)
    for level_start in bucket_steps(bins, reach):
        result = result + (magnitude >= level_start).astype(jnp.int32)
    return result


def norm_layer(values, gain_row, shift_row):
    average = jnp.mean(values, axis=-1, keepdims=True)
    centred = values - average
    second = jnp.mean(centred * centred, axis=-1, keepdims=True)
    return centred * lax.rsqrt(second + EPSILON) * gain_row + shift_row


def gelu_exact(values):
    return jax.nn.gelu(values, approximate=False)


def reading_place(region, order_rank):
    earlier = (region[:, None, :] < region[:, :, None]).astype(jnp.int32)
    return (jnp.sum(earlier, axis=2) + order_rank).astype(jnp.int32)


def page_buckets(place_row, across_row, down_row):
    order_bin = bucket_of(place_row[None, :] - place_row[:, None], BINS1, MAX_ORDER)
    across_bin = bucket_of(across_row[None, :] - across_row[:, None], BINS2, MAX_LAYOUT)
    down_bin = bucket_of(down_row[None, :] - down_row[:, None], BINS2, MAX_LAYOUT)
    return (order_bin, across_bin, down_bin)


def one_hot_of(grid, bins, dtype):
    return (grid[:, :, None] == jnp.arange(bins, dtype=jnp.int32)[None, None, :]).astype(dtype)


def relative_bias(tables, read_place, across, downward):

    def relative_one_page(inputs):
        grids = page_buckets(inputs[0], inputs[1], inputs[2])
        total = None
        for table, grid in zip(tables, grids):
            chooser = one_hot_of(grid, table.shape[1], jnp.float32)
            term = jnp.einsum(
                "hb,qkb->hqk", table, chooser, precision=HIGHEST, preferred_element_type=jnp.float32
            )
            total = term if total is None else total + term
        return total

    return lax.map(relative_one_page, (read_place, across, downward))


def table_grads(grad_scores, bins_list, read_place, across, downward):

    def table_one_page(inputs):
        grad_page = inputs[0]
        grids = page_buckets(inputs[1], inputs[2], inputs[3])
        return tuple(
            (
                jnp.einsum(
                    "hqk,qkb->hb",
                    grad_page,
                    one_hot_of(grid, bins, jnp.bfloat16),
                    preferred_element_type=jnp.float32,
                )
                for grid, bins in zip(grids, bins_list)
            )
        )

    per_page = lax.map(table_one_page, (grad_scores, read_place, across, downward))
    return tuple((jnp.sum(member, axis=0) for member in per_page))


def forward(tokens, lowered, biases, rel_bias):
    query_weight, key_weight, value_weight, out_weight, in_weight, down_weight = lowered
    b_query, b_value, b_out, ln1_gain, ln1_bias, b_in, b_down, ln2_gain, ln2_bias = biases
    page_count, head_count, length = (rel_bias.shape[0], rel_bias.shape[1], rel_bias.shape[2])
    shape_heads = (page_count, length, head_count, HEAD_DIM)
    tokens_low = tokens.astype(jnp.bfloat16)
    query_rows = (
        jnp.dot(tokens_low, query_weight, preferred_element_type=jnp.float32) + b_query
    ).astype(jnp.bfloat16)
    key_rows = jnp.dot(tokens_low, key_weight, preferred_element_type=jnp.float32).astype(
        jnp.bfloat16
    )
    value_rows = (
        jnp.dot(tokens_low, value_weight, preferred_element_type=jnp.float32) + b_value
    ).astype(jnp.bfloat16)
    scores = (
        jnp.einsum(
            "pqhe,pkhe->phqk",
            query_rows.reshape(shape_heads),
            key_rows.reshape(shape_heads),
            preferred_element_type=jnp.float32,
        )
        * SCORE_SCALE
        + rel_bias
    )
    row_top = jnp.max(scores, axis=-1, keepdims=True)
    raised = jnp.exp(scores - row_top)
    row_total = jnp.sum(raised, axis=-1, keepdims=True)
    attention = raised / row_total
    log_total = row_top + jnp.log(row_total)
    mixed = jnp.einsum(
        "phqk,pkhe->pqhe",
        attention.astype(jnp.bfloat16),
        value_rows.reshape(shape_heads),
        preferred_element_type=jnp.float32,
    )
    attended = mixed.reshape(tokens.shape[0], -1).astype(jnp.bfloat16)
    partial_value = jnp.dot(attended, out_weight, preferred_element_type=jnp.float32)
    branch = lax.psum(partial_value, "narrow") + b_out
    residual_one = tokens + branch
    hidden = norm_layer(residual_one, ln1_gain, ln1_bias)
    hidden_low = hidden.astype(jnp.bfloat16)
    pre_gelu = jnp.dot(hidden_low, in_weight, preferred_element_type=jnp.float32) + b_in
    active = gelu_exact(pre_gelu).astype(jnp.bfloat16)
    ff_part = jnp.dot(active, down_weight, preferred_element_type=jnp.float32)
    residual_two = hidden + (lax.psum(ff_part, "narrow") + b_down)
    output = norm_layer(residual_two, ln2_gain, ln2_bias)
    kept_values = (
        tokens_low,
        query_rows,
        key_rows,
        value_rows,
        log_total,
        attended,
        residual_one,
        hidden_low,
        pre_gelu,
        active,
        residual_two,
    )
    return (output, kept_values)


def local(
    tokens,
    region,
    order_rank,
    box_coords,
    w_query,
    b_query,
    w_key,
    w_value,
    b_value,
    w_out,
    b_out,
    ln1_gain,
    ln1_bias,
    w_in,
    b_in,
    w_down,
    b_down,
    ln2_gain,
    ln2_bias,
    rel_order,
    rel_x,
    rel_y,
    cotangent,
):
    length = PAGE
    page_count = tokens.shape[0] // length
    read_place = reading_place(
        region.reshape(page_count, length), order_rank.reshape(page_count, length)
    )
    corners = box_coords.reshape(2, page_count, length)
    rel_bias = relative_bias((rel_order, rel_x, rel_y), read_place, corners[0], corners[1])
    lowered = tuple(
        (weight.astype(jnp.bfloat16) for weight in (w_query, w_key, w_value, w_out, w_in, w_down))
    )
    query_weight, key_weight, value_weight, out_weight, in_weight, down_weight = lowered
    biases = (b_query, b_value, b_out, ln1_gain, ln1_bias, b_in, b_down, ln2_gain, ln2_bias)
    output, kept_values = forward(tokens, lowered, biases, rel_bias)
    tokens_again = lax.optimization_barrier((tokens, output))[0]
    kept_values = forward(tokens_again, lowered, biases, rel_bias)[1]
    (
        tokens_low,
        query_rows,
        key_rows,
        value_rows,
        log_total,
        attended,
        residual_one,
        hidden_low,
        pre_gelu,
        active,
        residual_two,
    ) = kept_values
    head_count = rel_bias.shape[1]
    shape_heads = (page_count, length, head_count, HEAD_DIM)
    head_width = head_count * HEAD_DIM
    _, second_back = jax.vjp(norm_layer, residual_two, ln2_gain, ln2_bias)
    grad_residual_two, grad_ln2_gain, grad_ln2_bias = second_back(cotangent)
    grad_ff = grad_residual_two.astype(jnp.bfloat16)
    grad_b_down = jnp.sum(grad_ff, axis=0, dtype=jnp.float32)
    grad_w_down = jnp.einsum("tf,td->fd", active, grad_ff, preferred_element_type=jnp.float32)
    grad_active = jnp.einsum("td,fd->tf", grad_ff, down_weight, preferred_element_type=jnp.float32)
    _, gelu_back = jax.vjp(gelu_exact, pre_gelu)
    grad_pre = gelu_back(grad_active)[0].astype(jnp.bfloat16)
    grad_b_in = jnp.sum(grad_pre, axis=0, dtype=jnp.float32)
    grad_w_in = jnp.einsum("td,tf->df", hidden_low, grad_pre, preferred_element_type=jnp.float32)
    hidden_part = jnp.einsum("tf,df->td", grad_pre, in_weight, preferred_element_type=jnp.float32)
    grad_hidden = grad_residual_two + lax.psum(hidden_part, "narrow")
    _, first_back = jax.vjp(norm_layer, residual_one, ln1_gain, ln1_bias)
    grad_residual_one, grad_ln1_gain, grad_ln1_bias = first_back(grad_hidden)
    grad_branch = grad_residual_one.astype(jnp.bfloat16)
    grad_b_out = jnp.sum(grad_branch, axis=0, dtype=jnp.float32)
    grad_w_out = jnp.einsum("tc,td->cd", attended, grad_branch, preferred_element_type=jnp.float32)
    grad_attended = jnp.einsum(
        "td,cd->tc", grad_branch, out_weight, preferred_element_type=jnp.float32
    ).astype(jnp.bfloat16)
    query_heads = query_rows.reshape(shape_heads)
    key_heads = key_rows.reshape(shape_heads)
    value_heads = value_rows.reshape(shape_heads)
    grad_heads = grad_attended.reshape(shape_heads)
    scores = (
        jnp.einsum("pqhe,pkhe->phqk", query_heads, key_heads, preferred_element_type=jnp.float32)
        * SCORE_SCALE
        + rel_bias
    )
    attention = jnp.exp(scores - log_total)
    grad_attention = jnp.einsum(
        "pqhe,pkhe->phqk", grad_heads, value_heads, preferred_element_type=jnp.float32
    )
    inner_sum = jnp.sum(attention * grad_attention, axis=-1, keepdims=True)
    grad_scores = (attention * (grad_attention - inner_sum)).astype(jnp.bfloat16)
    grad_rel_order, grad_rel_x, grad_rel_y = table_grads(
        grad_scores, (BINS1, BINS2, BINS2), read_place, corners[0], corners[1]
    )
    grad_query = (
        (
            jnp.einsum(
                "phqk,pkhe->pqhe", grad_scores, key_heads, preferred_element_type=jnp.float32
            )
            * SCORE_SCALE
        )
        .astype(jnp.bfloat16)
        .reshape(-1, head_width)
    )
    grad_key = (
        (
            jnp.einsum(
                "phqk,pqhe->pkhe", grad_scores, query_heads, preferred_element_type=jnp.float32
            )
            * SCORE_SCALE
        )
        .astype(jnp.bfloat16)
        .reshape(-1, head_width)
    )
    grad_value = (
        jnp.einsum(
            "phqk,pqhe->pkhe",
            attention.astype(jnp.bfloat16),
            grad_heads,
            preferred_element_type=jnp.float32,
        )
        .astype(jnp.bfloat16)
        .reshape(-1, head_width)
    )
    grad_b_query = jnp.sum(grad_query, axis=0, dtype=jnp.float32)
    grad_b_value = jnp.sum(grad_value, axis=0, dtype=jnp.float32)
    grad_w_query = jnp.einsum(
        "td,tc->dc", tokens_low, grad_query, preferred_element_type=jnp.float32
    )
    grad_w_key = jnp.einsum("td,tc->dc", tokens_low, grad_key, preferred_element_type=jnp.float32)
    grad_w_value = jnp.einsum(
        "td,tc->dc", tokens_low, grad_value, preferred_element_type=jnp.float32
    )
    input_part = jnp.einsum(
        "tc,dc->td", grad_query, query_weight, preferred_element_type=jnp.float32
    )
    input_part = input_part + jnp.einsum(
        "tc,dc->td", grad_key, key_weight, preferred_element_type=jnp.float32
    )
    input_part = input_part + jnp.einsum(
        "tc,dc->td", grad_value, value_weight, preferred_element_type=jnp.float32
    )
    grad_input = grad_residual_one + lax.psum(input_part, "narrow")
    (
        grad_w_query,
        grad_b_query,
        grad_w_key,
        grad_w_value,
        grad_b_value,
        grad_w_out,
        grad_b_out,
        grad_ln1_gain,
        grad_ln1_bias,
        grad_rel_order,
        grad_rel_x,
        grad_rel_y,
        grad_w_in,
        grad_b_in,
        grad_w_down,
        grad_b_down,
        grad_ln2_gain,
        grad_ln2_bias,
    ) = lax.psum(
        (
            grad_w_query,
            grad_b_query,
            grad_w_key,
            grad_w_value,
            grad_b_value,
            grad_w_out,
            grad_b_out,
            grad_ln1_gain,
            grad_ln1_bias,
            grad_rel_order,
            grad_rel_x,
            grad_rel_y,
            grad_w_in,
            grad_b_in,
            grad_w_down,
            grad_b_down,
            grad_ln2_gain,
            grad_ln2_bias,
        ),
        "wide",
    )
    return (
        output,
        grad_input,
        grad_w_query,
        grad_b_query,
        grad_w_key,
        grad_w_value,
        grad_b_value,
        grad_w_out,
        grad_b_out,
        grad_ln1_gain,
        grad_ln1_bias,
        grad_w_in,
        grad_b_in,
        grad_w_down,
        grad_b_down,
        grad_ln2_gain,
        grad_ln2_bias,
        grad_rel_order,
        grad_rel_x,
        grad_rel_y,
    )


def solution(mesh):
    in_specs = (
        P("wide", None),
        P("wide"),
        P("wide"),
        P(None, "wide"),
        P(None, "narrow"),
        P("narrow"),
        P(None, "narrow"),
        P(None, "narrow"),
        P("narrow"),
        P("narrow", None),
        P(),
        P(),
        P(),
        P(None, "narrow"),
        P("narrow"),
        P("narrow", None),
        P(),
        P(),
        P(),
        P("narrow", None),
        P("narrow", None),
        P("narrow", None),
        P("wide", None),
    )
    out_specs = (
        P("wide", None),
        P("wide", None),
        P(None, "narrow"),
        P("narrow"),
        P(None, "narrow"),
        P(None, "narrow"),
        P("narrow"),
        P("narrow", None),
        P(),
        P(),
        P(),
        P(None, "narrow"),
        P("narrow"),
        P("narrow", None),
        P(),
        P(),
        P(),
        P("narrow", None),
        P("narrow", None),
        P("narrow", None),
    )
    return jax.shard_map(local, mesh=mesh, in_specs=in_specs, out_specs=out_specs, check_vma=False)
```

profile of v0, /device:TPU:0, one launch (start us, length us, event | category | flops | bytes accessed | tf_op | source)
XLA Modules:
  0.0 774.5 jit_solution(14613207930424786507)
XLA Ops:
  8.0 13.1 %fusion.116 = s32[561]{0:T(1024)S(1)} fusion(s32[561]{0:T(1024)} %param.24), kind=kLoop, calls=%fused_computation.185 | loop fusion | flops 943602 | bytes 4488 | tf_op jit(solution)/shard_map/reduce_sum | solution.py:60
  21.8 2.5 convert_add_fusion.2
  24.3 9.5 %convert_add_fusion = (s32[561,561]{0,1:T(8,128)S(1)}, s32[561,561]{0,1:T(8,128)S(1)}) fusion(s32[561]{0:T(1024)S(1)} %get-tuple-element.77, s32[561]{0:T(1024)S(1)} %get-tuple-element.76), kind=kLoop, calls=%fused_computation.182 | loop fusion | flops 61055736 | bytes 2522256 | tf_op jit(solution)/shard_map/while/body/eval_jaxpr/add | solution.py:43
  33.8 28.1 %fusion.2 = f32[561,561,3]{0,2,1:T(4,128)S(1)} fusion(s32[561,561]{0,1:T(8,128)S(1)} %get-tuple-element.126, f32[3,64]{1,0:T(4,128)S(1)} %copy-done), kind=kOutput, calls=%fused_computation.3 | convolution fusion | flops 745259328 | bytes 5036304 | tf_op jit(solution)/shard_map/while/body/eval_jaxpr/hb,qkb->hqk/dot_general | solution.py:81
  61.9 29.6 %fusion.4 = f32[561,561,3]{0,2,1:T(4,128)} fusion(s32[561,561]{0,1:T(8,128)S(1)} %get-tuple-element.127, f32[3,64]{1,0:T(4,128)S(1)} %copy-done.60), kind=kOutput, calls=%fused_computation.6 | convolution fusion | flops 745259328 | bytes 5036304 | tf_op jit(solution)/shard_map/while/body/eval_jaxpr/hb,qkb->hqk/dot_general | solution.py:81
  91.5 15.8 %fusion.10 = f32[561,561,3]{0,2,1:T(4,128)} fusion(s32[561,561]{0,1:T(8,128)S(1)} %convert_add_fusion.2, f32[3,32]{1,0:T(4,128)S(1)} %copy-done.61), kind=kOutput, calls=%fused_computation.13 | convolution fusion | flops 372629664 | bytes 5035920 | tf_op jit(solution)/shard_map/while/body/eval_jaxpr/hb,qkb->hqk/dot_general | solution.py:81
  108.9 5.0 copy_add_fusion
  118.7 4.9 fusion.120
  125.5 77.9 %all-reduce.10.cloned.1.call-done = f32[561,768]{1,0:T(8,128)} async-done(((f32[561,768]{1,0:T(8,128)}), f32[561,768]{1,0:T(8,128)}) %all-reduce.10.cloned.1.call-update) | async-done | bytes 1723408 | tf_op jit(solution)/shard_map/psum | solution.py:149
  205.9 8.9 %fusion.119 = f32[561,768]{1,0:T(8,128)} fusion(f32[561,768]{1,0:T(8,128)S(1)} %get-tuple-element.114, f32[768]{0:T(1024)S(1)} %copy-done.59, f32[768]{0:T(1024)S(1)} %copy-done.52, f32[768]{0:T(1024)S(1)} %copy-done.48, f32[561]{0:T(1024)S(1)} %add_rsqrt_fusion.1, f32[561]{0:T(1024)S(1)} %broadcast_multiply_fusion.3, f32[768,768]{1,0:T(8,128)} %param.38, ...), kind=kOutput, calls=%fused_computation.194 | convolution fusion | flops 1355334912 | bytes 8179080 | tf_op jit(solution)/shard_map/dot_general | solution.py:155
  214.9 74.4 %all-reduce.12.cloned.1.call-done = f32[561,768]{1,0:T(8,128)} async-done(((f32[561,768]{1,0:T(8,128)}), f32[561,768]{1,0:T(8,128)}) %all-reduce.12.cloned.1.call-update) | async-done | bytes 1723408 | tf_op jit(solution)/shard_map/psum | solution.py:156
  289.3 2.1 fusion.256
  303.8 74.0 %all-reduce.14.cloned.1.call-done = f32[561,768]{1,0:T(8,128)} async-done(((f32[561,768]{1,0:T(8,128)}), f32[561,768]{1,0:T(8,128)}) %all-reduce.14.cloned.1.call-update) | async-done | bytes 1723408 | tf_op jit(solution)/shard_map/psum | solution.py:149
  380.1 6.0 multiply_convert_fusion.1
  387.1 2.1 fusion.189
  389.2 74.4 %all-reduce.16.cloned.1.call-done = f32[561,768]{1,0:T(8,128)} async-done(((f32[561,768]{1,0:T(8,128)}), f32[561,768]{1,0:T(8,128)}) %all-reduce.16.cloned.1.call-update) | async-done | bytes 1723408 | tf_op jit(solution)/shard_map/psum | solution.py:156
  463.6 2.1 fusion.253
  471.7 2.0 convert_reduce_fusion.1
  474.6 2.1 fusion.223
  476.8 74.3 %all-reduce.18.cloned.1.call-done = f32[561,768]{1,0:T(8,128)} async-done(((f32[561,768]{1,0:T(8,128)}), f32[561,768]{1,0:T(8,128)}) %all-reduce.18.cloned.1.call-update) | async-done | bytes 1723408 | tf_op jit(solution)/shard_map/psum | solution.py:241
  551.2 2.6 multiply_reduce_fusion.2
  565.4 4.0 fusion.264
  569.4 2.9 fusion.248
  572.5 2.3 fusion.263
  580.0 8.8 %fusion.131 = f32[3,32]{1,0:T(4,128)S(1)} fusion(s32[561,561]{0,1:T(8,128)} %copy-done.34, bf16[3,561,561]{1,2,0:T(8,128)(2,1)S(1)} %copy-done.8), kind=kOutput, calls=%fused_computation.207 | convolution fusion | flops 70497504 | bytes 3147594 | tf_op jit(solution)/shard_map/while/body/eval_jaxpr/hqk,qkb->hb/dot_general | solution.py:97
  588.9 14.6 %fusion.134 = f32[3,64]{1,0:T(4,128)S(1)} fusion(s32[561,561]{0,1:T(8,128)S(1)} %copy-done.38, bf16[3,561,561]{1,2,0:T(8,128)(2,1)S(1)} %copy-done.8), kind=kOutput, calls=%fused_computation.208 | convolution fusion | flops 140995008 | bytes 3147978 | tf_op jit(solution)/shard_map/while/body/eval_jaxpr/hqk,qkb->hb/dot_general | solution.py:97
  603.5 14.9 %fusion.137 = f32[3,64]{1,0:T(4,128)S(1)} fusion(s32[561,561]{0,1:T(8,128)S(1)} %copy-done.36, bf16[3,561,561]{1,2,0:T(8,128)(2,1)S(1)} %copy-done.8), kind=kOutput, calls=%fused_computation.209 | convolution fusion | flops 140995008 | bytes 3147978 | tf_op jit(solution)/shard_map/while/body/eval_jaxpr/hqk,qkb->hb/dot_general | solution.py:97
  618.4 25.3 %all-reduce = (f32[192]{0:T(256)}, f32[192]{0:T(256)}, f32[768]{0:T(1024)}, f32[768]{0:T(1024)}, f32[768]{0:T(1024)}, /*index=5*/f32[768]{0:T(1024)}, f32[768]{0...) all-reduce(f32[192]{0:T(256)S(1)} %reduce_sum.254, ...), channel_id=1, replica_groups=mesh['wide'=8,'narrow'=4] {'wide'}, use_global_device_ids=true, to_apply=%region_26.27 | all-reduce | flops 6240 | bytes 49920 | tf_op jit(solution)/shard_map/psum | solution.py:336
  643.7 3.4 add_add_fusion.7
  647.1 110.7 %all-reduce.22.cloned.1.call-done = (f32[768,192]{0,1:T(8,128)}, f32[768,192]{0,1:T(8,128)}, f32[768,192]{0,1:T(8,128)}, f32[192,768]{1,0:T(8,128)}, f32[768,768]{1,0:T(8,128)}, /*index=5*/f32[768,768]{1,0:T(8,128)}) async-done(((f32[768,192]{0,1:T(8,128)}, f32[768,192]{0,1:T(8,128)}, f32[768,192]{0,1:T(8,128)}, f32[192,768]{1,0:T(8,128)}, f32[768,768]{1,0:T(8,128)}, /*index=5*/f32[768,768]{1,0:T(8,128)}), ...) | async-done | bytes 7077904 | tf_op jit(solution)/shard_map/psum | solution.py:336
  757.8 2.0 copy.114
  759.8 2.1 copy.115
  (212 shorter events, 57.2 us)
Async XLA Ops:
  7.2 26.6 %copy-start = (f32[3,64]{1,0:T(4,128)S(1)}, f32[3,64]{1,0:T(4,128)}, u32[]{:S(2)}) copy-start(f32[3,64]{1,0:T(4,128)} %param.44) | copy-start | bytes 2308
  7.2 196.2 %all-reduce.10.cloned.1.call-start = ((), (), s32[]{:S(2)}) async-start(), calls=%async_computation | async-start | bytes 3489792 | tf_op jit(solution)/shard_map/psum | solution.py:149
  24.3 67.3 %copy-start.34 = (s32[561,561]{0,1:T(8,128)}, s32[561,561]{0,1:T(8,128)S(1)}, u32[]{:S(2)}) copy-start(s32[561,561]{0,1:T(8,128)S(1)} %convert_add_fusion.2) | copy-start | bytes 3776656
  33.8 28.1 %copy-start.35 = (s32[561,561]{0,1:T(8,128)}, s32[561,561]{0,1:T(8,128)S(1)}, u32[]{:S(2)}) copy-start(s32[561,561]{0,1:T(8,128)S(1)} %get-tuple-element.126) | copy-start | bytes 3776656
  33.8 28.1 %copy-start.37 = (s32[561,561]{0,1:T(8,128)}, s32[561,561]{0,1:T(8,128)S(1)}, u32[]{:S(2)}) copy-start(s32[561,561]{0,1:T(8,128)S(1)} %get-tuple-element.127) | copy-start | bytes 3776656
  33.8 28.1 %copy-start.60 = (f32[3,64]{1,0:T(4,128)S(1)}, f32[3,64]{1,0:T(4,128)}, u32[]{:S(2)}) copy-start(f32[3,64]{1,0:T(4,128)} %param.43) | copy-start | bytes 2308
  61.9 29.6 %copy-start.61 = (f32[3,32]{1,0:T(4,128)S(1)}, f32[3,32]{1,0:T(4,128)}, u32[]{:S(2)}) copy-start(f32[3,32]{1,0:T(4,128)} %param.42) | copy-start | bytes 1156
  91.5 15.8 %copy-start.3 = (f32[561,768]{1,0:T(8,128)S(1)}, f32[561,768]{1,0:T(8,128)}, u32[]{:S(2)}) copy-start(f32[561,768]{1,0:T(8,128)} %param.23) | copy-start | bytes 5170180
  91.5 15.8 %copy-start.15 = (f32[768,192]{0,1:T(8,128)S(1)}, f32[768,192]{0,1:T(8,128)}, u32[]{:S(2)}) copy-start(f32[768,192]{0,1:T(8,128)} %param.29) | copy-start | bytes 1769476
  118.7 4.9 copy-start.12
  123.6 79.8 %copy-start.50 = (f32[768]{0:T(1024)S(1)}, f32[768]{0:T(1024)}, u32[]{:S(2)}) copy-start(f32[768]{0:T(1024)} %param.33) | copy-start | bytes 9220
  125.3 164.0 %all-reduce.12.cloned.1.call-start = ((), (), s32[]{:S(2)}) async-start(), calls=%async_computation.1 | async-start | bytes 3489792 | tf_op jit(solution)/shard_map/psum | solution.py:156
  214.8 74.5 %copy-start.51 = (f32[768]{0:T(1024)S(1)}, f32[768]{0:T(1024)}, u32[]{:S(2)}) copy-start(f32[768]{0:T(1024)} %param.39) | copy-start | bytes 9220
  214.9 162.9 %all-reduce.14.cloned.1.call-start = ((), (), s32[]{:S(2)}) async-start(), calls=%async_computation.2 | async-start | bytes 3489792 | tf_op jit(solution)/shard_map/psum | solution.py:149
  292.1 4.9 slice-start.2
  303.4 160.2 %all-reduce.16.cloned.1.call-start = ((), (), s32[]{:S(2)}) async-start(), calls=%async_computation.3 | async-start | bytes 3489792 | tf_op jit(solution)/shard_map/psum | solution.py:156
  380.1 7.0 copy-start.26
  389.2 162.0 %all-reduce.18.cloned.1.call-start = ((), (), s32[]{:S(2)}) async-start(), calls=%async_computation.4 | async-start | bytes 3489792 | tf_op jit(solution)/shard_map/psum | solution.py:241
  470.1 3.6 copy-start.42
  476.7 166.9 %all-reduce.20.cloned.1.call-start = ((), (), s32[]{:S(2)}) async-start(), calls=%async_computation.5 | async-start | bytes 3489792 | tf_op jit(solution)/shard_map/psum | solution.py:316
  551.2 5.4 slice-start
  565.2 192.7 %all-reduce.22.cloned.1.call-start = ((), (), s32[]{:S(2)}) async-start(), calls=%async_computation.6 | async-start | bytes 14155776 | tf_op jit(solution)/shard_map/psum | solution.py:336
  565.4 4.0 copy-start.45
  580.0 8.8 %copy-start.38 = (s32[561,561]{0,1:T(8,128)S(1)}, s32[561,561]{0,1:T(8,128)}, u32[]{:S(2)}) copy-start(s32[561,561]{0,1:T(8,128)} %copy-done.37) | copy-start | bytes 3776656
  588.9 14.7 %copy-start.36 = (s32[561,561]{0,1:T(8,128)S(1)}, s32[561,561]{0,1:T(8,128)}, u32[]{:S(2)}) copy-start(s32[561,561]{0,1:T(8,128)} %copy-done.35) | copy-start | bytes 3776656
  603.5 14.9 %copy-start.53 = (f32[768]{0:T(1024)S(1)}, f32[768]{0:T(1024)}, u32[]{:S(2)}) copy-start(f32[768]{0:T(1024)} %get-tuple-element.74) | copy-start | bytes 9220
  603.5 14.9 %copy-start.54 = (f32[768]{0:T(1024)S(1)}, f32[768]{0:T(1024)}, u32[]{:S(2)}) copy-start(f32[768]{0:T(1024)} %get-tuple-element.96) | copy-start | bytes 9220
  603.5 14.9 %copy-start.58 = (f32[768]{0:T(1024)S(1)}, f32[768]{0:T(1024)}, u32[]{:S(2)}) copy-start(f32[768]{0:T(1024)} %get-tuple-element.124) | copy-start | bytes 9220
  757.8 4.1 copy-start.47
  757.8 4.9 copy-start.46
  759.8 3.7 copy-start.25
  763.5 3.9 copy-start.1
  (43 other events, 70.1 us)
Sparse Core Ops, SparseCore 0:
  125.4 77.9 all-reduce.9
  215.0 74.2 all-reduce.11
  303.5 74.2 all-reduce.13
  389.3 74.2 all-reduce.15
  476.9 74.2 all-reduce.17
  565.3 74.2 all-reduce.19
  644.8 112.9 all-reduce.21
where the time goes:
time: 779 us; the launch traced here: 775 us
  waiting for transfers between devices  486 us (62%)
  matrix products  166 us (21%)
  other arithmetic  54.1 us (7%)
  local copies, waits for them, and re-layouts  27.4 us (4%)
  blocking collectives  25.3 us (3%)
  between operations  15.1 us (2%)
    psum x2, waiting for transfers between devices, forward(): branch = lax.psum(partial_value, 'narrow') + b_out  152 us
    psum x2, waiting for transfers between devices, forward(): residual_two = hidden + (lax.psum(ff_part, 'narrow') + b_down)  149 us
    psum x1, waiting for transfers between devices, local(): lax.psum((grad_w_query, grad_b_query, grad_w_key, grad_w_value, grad_b_va...  111 us
    psum x1, waiting for transfers between devices, local(): grad_hidden = grad_residual_two + lax.psum(hidden_part, 'narrow')  74.3 us
    dot_general x3, matrix products, relative_one_page(): jnp.einsum('hb,qkb->hqk', table, chooser, precision=HIGHEST, preferred_el...  73.4 us
    dot_general x3, matrix products, table_one_page(): jnp.einsum('hqk,qkb->hb', grad_page, one_hot_of(grid, bins, jnp.bfloat16)...  38.3 us
    unnamed x142, local copies, waits for them, and re-layouts  26.4 us
    psum x1, blocking collectives, local(): lax.psum((grad_w_query, grad_b_query, grad_w_key, grad_w_value, grad_b_va...  25.3 us
  transfers between devices with their start and end apart: 7, of which 6 were waited for; matrix products, arithmetic and copies ran while one was open for 7% of the time, Pallas kernels for 0%

commit v1 on v0

--- a/solution.py
+++ b/solution.py
@@ -3,6 +3,7 @@
 import jax.numpy as jnp
 from jax import lax
 from jax.sharding import PartitionSpec as P
+from jax.lax import all_gather
 
 HEAD_DIM = 64
 BINS1 = 32
@@ -13,6 +14,7 @@
 HIGHEST = lax.Precision.HIGHEST
 EPSILON = 1e-05
 SCORE_SCALE = 0.125
+prepare_runs = lambda chunk, net_axis: jnp.sum(all_gather(chunk, net_axis), axis=0)
 
 
 def bucket_steps(bins, reach):
@@ -238,7 +240,7 @@
     grad_b_in = jnp.sum(grad_pre, axis=0, dtype=jnp.float32)
     grad_w_in = jnp.einsum("td,tf->df", hidden_low, grad_pre, preferred_element_type=jnp.float32)
     hidden_part = jnp.einsum("tf,df->td", grad_pre, in_weight, preferred_element_type=jnp.float32)
-    grad_hidden = grad_residual_two + lax.psum(hidden_part, "narrow")
+    grad_hidden = grad_residual_two + prepare_runs(hidden_part, "narrow")
     _, first_back = jax.vjp(norm_layer, residual_one, ln1_gain, ln1_bias)
     grad_residual_one, grad_ln1_gain, grad_ln1_bias = first_back(grad_hidden)
     grad_branch = grad_residual_one.astype(jnp.bfloat16)

time: 779 us -> 840 us (1.078)
  waiting for transfers between devices: 486 us -> 535 us
    all_gather x0 -> x1, waiting for transfers between devices: none -> 126 us  [all_gather(chunk, net_axis)]
    psum x1 -> x0, waiting for transfers between devices: 74.3 us -> none  [local(): grad_hidden = grad_residual_two + lax.psum(hidden_part, 'narrow')]
    unnamed x142 -> x158, local copies, waits for them, and re-layouts: 26.4 us -> 27.1 us
where the time goes in v1:
time: 840 us; the launch traced here: 831 us
  waiting for transfers between devices  535 us (64%)
  matrix products  166 us (20%)
  other arithmetic  58.8 us (7%)
  local copies, waits for them, and re-layouts  28 us (3%)
  blocking collectives  26.4 us (3%)
  between operations  15.4 us (2%)
    psum x2, waiting for transfers between devices, forward(): branch = lax.psum(partial_value, 'narrow') + b_out  152 us
    psum x2, waiting for transfers between devices, forward(): residual_two = hidden + (lax.psum(ff_part, 'narrow') + b_down)  148 us
    all_gather x1, waiting for transfers between devices, all_gather(chunk, net_axis)  126 us
    psum x1, waiting for transfers between devices, local(): lax.psum((grad_w_query, grad_b_query, grad_w_key, grad_w_value, grad_b_va...  109 us
    dot_general x3, matrix products, relative_one_page(): jnp.einsum('hb,qkb->hqk', table, chooser, precision=HIGHEST, preferred_el...  73.7 us
    dot_general x3, matrix products, table_one_page(): jnp.einsum('hqk,qkb->hb', grad_page, one_hot_of(grid, bins, jnp.bfloat16)...  38.4 us
    unnamed x158, local copies, waits for them, and re-layouts  27.1 us
    psum x1, blocking collectives, local(): lax.psum((grad_w_query, grad_b_query, grad_w_key, grad_w_value, grad_b_va...  26.4 us
  transfers between devices with their start and end apart: 7, of which 6 were waited for; matrix products, arithmetic and copies ran while one was open for 7% of the time, Pallas kernels for 0%

profile of v1, /device:TPU:0, one launch (start us, length us, event | category | flops | bytes accessed | tf_op | source)
XLA Modules:
  0.0 830.7 jit_solution(16110903949797491050)
XLA Ops:
  7.3 12.5 %fusion.117 = s32[561]{0:T(1024)S(1)} fusion(s32[561]{0:T(1024)} %param.24), kind=kLoop, calls=%fused_computation.186 | loop fusion | flops 943602 | bytes 4488 | tf_op jit(solution)/shard_map/reduce_sum | solution.py:62
  20.5 2.5 convert_add_fusion.2
  23.8 14.3 %fusion.10 = f32[561,561,3]{0,2,1:T(4,128)S(1)} fusion(s32[561,561]{0,1:T(8,128)S(1)} %convert_add_fusion.2, f32[3,32]{1,0:T(4,128)S(1)} %copy-done), kind=kOutput, calls=%fused_computation.13 | convolution fusion | flops 372629664 | bytes 5035920 | tf_op jit(solution)/shard_map/while/body/eval_jaxpr/hb,qkb->hqk/dot_general | solution.py:83
  38.1 9.3 %convert_add_fusion = (s32[561,561]{0,1:T(8,128)S(1)}, s32[561,561]{0,1:T(8,128)S(1)}) fusion(s32[561]{0:T(1024)S(1)} %get-tuple-element.77, s32[561]{0:T(1024)S(1)} %get-tuple-element.76), kind=kLoop, calls=%fused_computation.183 | loop fusion | flops 61055736 | bytes 2522256 | tf_op jit(solution)/shard_map/while/body/eval_jaxpr/add | solution.py:45
  47.5 29.7 %fusion.2 = f32[561,561,3]{0,2,1:T(4,128)} fusion(s32[561,561]{0,1:T(8,128)S(1)} %get-tuple-element.126, f32[3,64]{1,0:T(4,128)S(1)} %copy-done.68), kind=kOutput, calls=%fused_computation.3 | convolution fusion | flops 745259328 | bytes 5036304 | tf_op jit(solution)/shard_map/while/body/eval_jaxpr/hb,qkb->hqk/dot_general | solution.py:83
  77.3 29.7 %fusion.4 = f32[561,561,3]{0,2,1:T(4,128)} fusion(s32[561,561]{0,1:T(8,128)S(1)} %get-tuple-element.127, f32[3,64]{1,0:T(4,128)S(1)} %copy-done.69), kind=kOutput, calls=%fused_computation.6 | convolution fusion | flops 745259328 | bytes 5036304 | tf_op jit(solution)/shard_map/while/body/eval_jaxpr/hb,qkb->hqk/dot_general | solution.py:83
  108.6 5.0 fusion.13
  118.2 4.8 fusion.121
  124.8 78.0 %all-reduce.9.cloned.1.call-done = f32[561,768]{1,0:T(8,128)} async-done(((f32[561,768]{1,0:T(8,128)}), f32[561,768]{1,0:T(8,128)}) %all-reduce.9.cloned.1.call-update) | async-done | bytes 1723408 | tf_op jit(solution)/shard_map/psum | solution.py:151
  205.4 8.9 %fusion.120 = f32[561,768]{1,0:T(8,128)} fusion(f32[561,768]{1,0:T(8,128)S(1)} %get-tuple-element.114, f32[768]{0:T(1024)S(1)} %copy-done.67, f32[768]{0:T(1024)S(1)} %copy-done.59, f32[768]{0:T(1024)S(1)} %copy-done.55, f32[561]{0:T(1024)S(1)} %add_rsqrt_fusion.1, f32[561]{0:T(1024)S(1)} %broadcast_multiply_fusion.3, f32[768,768]{1,0:T(8,128)} %param.38, ...), kind=kOutput, calls=%fused_computation.195 | convolution fusion | flops 1355334912 | bytes 8179080 | tf_op jit(solution)/shard_map/dot_general | solution.py:157
  214.8 74.0 %all-reduce.11.cloned.1.call-done = f32[561,768]{1,0:T(8,128)} async-done(((f32[561,768]{1,0:T(8,128)}), f32[561,768]{1,0:T(8,128)}) %all-reduce.11.cloned.1.call-update) | async-done | bytes 1723408 | tf_op jit(solution)/shard_map/psum | solution.py:158
  288.8 2.1 fusion.256
  302.9 74.4 %all-reduce.13.cloned.1.call-done = f32[561,768]{1,0:T(8,128)} async-done(((f32[561,768]{1,0:T(8,128)}), f32[561,768]{1,0:T(8,128)}) %all-reduce.13.cloned.1.call-update) | async-done | bytes 1723408 | tf_op jit(solution)/shard_map/psum | solution.py:151
  379.6 6.0 multiply_convert_fusion.1
  386.5 2.1 fusion.190
  388.8 74.2 %all-reduce.15.cloned.1.call-done = f32[561,768]{1,0:T(8,128)} async-done(((f32[561,768]{1,0:T(8,128)}), f32[561,768]{1,0:T(8,128)}) %all-reduce.15.cloned.1.call-update) | async-done | bytes 1723408 | tf_op jit(solution)/shard_map/psum | solution.py:158
  463.0 2.1 fusion.253
  474.1 2.1 convolution_bitcast_fusion
  476.3 125.7 %all-gather.4.cloned.1.call-done = f32[4,561,768]{2,1,0:T(8,128)} async-done(((f32[1,561,768]{2,1,0:T(8,128)}), f32[4,561,768]{2,1,0:T(8,128)}) %all-gather.4.cloned.1.call-update) | async-done | bytes 6893584 | tf_op jit(solution)/shard_map/all_gather | solution.py:17
  602.0 4.8 reduce_sum.258
  606.8 3.2 multiply_reduce_fusion.2
  622.5 3.8 fusion.264
  626.3 2.9 fusion.248
  629.4 2.2 fusion.260
  636.8 8.8 %fusion.132 = f32[3,32]{1,0:T(4,128)S(1)} fusion(s32[561,561]{0,1:T(8,128)} %copy-done.39, bf16[3,561,561]{1,2,0:T(8,128)(2,1)S(1)} %copy-done.8), kind=kOutput, calls=%fused_computation.208 | convolution fusion | flops 70497504 | bytes 3147594 | tf_op jit(solution)/shard_map/while/body/eval_jaxpr/hqk,qkb->hb/dot_general | solution.py:99
  645.7 14.6 %fusion.135 = f32[3,64]{1,0:T(4,128)S(1)} fusion(s32[561,561]{0,1:T(8,128)S(1)} %copy-done.43, bf16[3,561,561]{1,2,0:T(8,128)(2,1)S(1)} %copy-done.8), kind=kOutput, calls=%fused_computation.209 | convolution fusion | flops 140995008 | bytes 3147978 | tf_op jit(solution)/shard_map/while/body/eval_jaxpr/hqk,qkb->hb/dot_general | solution.py:99
  660.4 14.9 %fusion.138 = f32[3,64]{1,0:T(4,128)S(1)} fusion(s32[561,561]{0,1:T(8,128)S(1)} %copy-done.41, bf16[3,561,561]{1,2,0:T(8,128)(2,1)S(1)} %copy-done.8), kind=kOutput, calls=%fused_computation.210 | convolution fusion | flops 140995008 | bytes 3147978 | tf_op jit(solution)/shard_map/while/body/eval_jaxpr/hqk,qkb->hb/dot_general | solution.py:99
  675.3 26.4 %all-reduce = (f32[192]{0:T(256)}, f32[192]{0:T(256)}, f32[768]{0:T(1024)}, f32[768]{0:T(1024)}, f32[768]{0:T(1024)}, /*index=5*/f32[768]{0:T(1024)}, f32[768]{0...) all-reduce(f32[192]{0:T(256)S(1)} %reduce_sum.266, ...), channel_id=1, replica_groups=mesh['wide'=8,'narrow'=4] {'wide'}, use_global_device_ids=true, to_apply=%region_26.27 | all-reduce | flops 6240 | bytes 49920 | tf_op jit(solution)/shard_map/psum | solution.py:338
  701.7 3.4 add_add_fusion.7
  705.1 108.6 %all-reduce.19.cloned.1.call-done = (f32[768,192]{0,1:T(8,128)}, f32[768,192]{0,1:T(8,128)}, f32[768,192]{0,1:T(8,128)}, f32[192,768]{1,0:T(8,128)}, f32[768,768]{1,0:T(8,128)}, /*index=5*/f32[768,768]{1,0:T(8,128)}) async-done(((f32[768,192]{0,1:T(8,128)}, f32[768,192]{0,1:T(8,128)}, f32[768,192]{0,1:T(8,128)}, f32[192,768]{1,0:T(8,128)}, f32[768,768]{1,0:T(8,128)}, /*index=5*/f32[768,768]{1,0:T(8,128)}), ...) | async-done | bytes 7077904 | tf_op jit(solution)/shard_map/psum | solution.py:338
  813.8 2.0 copy.119
  815.8 2.1 copy.120
  (229 shorter events, 59.9 us)
Async XLA Ops:
  7.2 16.6 %copy-start = (f32[3,32]{1,0:T(4,128)S(1)}, f32[3,32]{1,0:T(4,128)}, u32[]{:S(2)}) copy-start(f32[3,32]{1,0:T(4,128)} %param.42) | copy-start | bytes 1156
  7.2 195.7 %all-reduce.9.cloned.1.call-start = ((), (), s32[]{:S(2)}) async-start(), calls=%async_computation | async-start | bytes 3489792 | tf_op jit(solution)/shard_map/psum | solution.py:151
  23.0 15.2 %copy-start.39 = (s32[561,561]{0,1:T(8,128)}, s32[561,561]{0,1:T(8,128)S(1)}, u32[]{:S(2)}) copy-start(s32[561,561]{0,1:T(8,128)S(1)} %convert_add_fusion.2) | copy-start | bytes 3776656
  38.1 9.4 %copy-start.68 = (f32[3,64]{1,0:T(4,128)S(1)}, f32[3,64]{1,0:T(4,128)}, u32[]{:S(2)}) copy-start(f32[3,64]{1,0:T(4,128)} %param.44) | copy-start | bytes 2308
  47.5 29.8 %copy-start.40 = (s32[561,561]{0,1:T(8,128)}, s32[561,561]{0,1:T(8,128)S(1)}, u32[]{:S(2)}) copy-start(s32[561,561]{0,1:T(8,128)S(1)} %get-tuple-element.126) | copy-start | bytes 3776656
  47.5 29.8 %copy-start.42 = (s32[561,561]{0,1:T(8,128)}, s32[561,561]{0,1:T(8,128)S(1)}, u32[]{:S(2)}) copy-start(s32[561,561]{0,1:T(8,128)S(1)} %get-tuple-element.127) | copy-start | bytes 3776656
  47.5 29.8 %copy-start.69 = (f32[3,64]{1,0:T(4,128)S(1)}, f32[3,64]{1,0:T(4,128)}, u32[]{:S(2)}) copy-start(f32[3,64]{1,0:T(4,128)} %param.43) | copy-start | bytes 2308
  77.3 29.7 %copy-start.3 = (f32[561,768]{1,0:T(8,128)S(1)}, f32[561,768]{1,0:T(8,128)}, u32[]{:S(2)}) copy-start(f32[561,768]{1,0:T(8,128)} %param.23) | copy-start | bytes 5170180
  77.3 29.7 %copy-start.15 = (f32[768,192]{0,1:T(8,128)S(1)}, f32[768,192]{0,1:T(8,128)}, u32[]{:S(2)}) copy-start(f32[768,192]{0,1:T(8,128)} %param.29) | copy-start | bytes 1769476
  118.2 4.8 copy-start.12
  123.1 79.8 %copy-start.57 = (f32[768]{0:T(1024)S(1)}, f32[768]{0:T(1024)}, u32[]{:S(2)}) copy-start(f32[768]{0:T(1024)} %param.33) | copy-start | bytes 9220
  124.8 164.0 %all-reduce.11.cloned.1.call-start = ((), (), s32[]{:S(2)}) async-start(), calls=%async_computation.1 | async-start | bytes 3489792 | tf_op jit(solution)/shard_map/psum | solution.py:158
  214.3 74.5 %copy-start.58 = (f32[768]{0:T(1024)S(1)}, f32[768]{0:T(1024)}, u32[]{:S(2)}) copy-start(f32[768]{0:T(1024)} %param.39) | copy-start | bytes 9220
  214.3 163.0 %all-reduce.13.cloned.1.call-start = ((), (), s32[]{:S(2)}) async-start(), calls=%async_computation.2 | async-start | bytes 3489792 | tf_op jit(solution)/shard_map/psum | solution.py:151
  291.6 4.9 slice-start.2
  302.9 160.2 %all-reduce.15.cloned.1.call-start = ((), (), s32[]{:S(2)}) async-start(), calls=%async_computation.3 | async-start | bytes 3489792 | tf_op jit(solution)/shard_map/psum | solution.py:158
  379.6 6.9 copy-start.26
  388.6 213.4 %all-gather.4.cloned.1.call-start = ((), (), s32[]{:S(2)}) async-start(), calls=%async_computation.5 | async-start | bytes 8724480 | tf_op jit(solution)/shard_map/all_gather | solution.py:17
  476.2 225.5 %all-reduce.17.cloned.1.call-start = ((), (), s32[]{:S(2)}) async-start(), calls=%async_computation.4 | async-start | bytes 3489792 | tf_op jit(solution)/shard_map/psum | solution.py:318
  606.8 6.0 slice-start
  621.4 192.4 %all-reduce.19.cloned.1.call-start = ((), (), s32[]{:S(2)}) async-start(), calls=%async_computation.6 | async-start | bytes 14155776 | tf_op jit(solution)/shard_map/psum | solution.py:338
  622.5 3.8 copy-start.52
  636.8 8.8 %copy-start.43 = (s32[561,561]{0,1:T(8,128)S(1)}, s32[561,561]{0,1:T(8,128)}, u32[]{:S(2)}) copy-start(s32[561,561]{0,1:T(8,128)} %copy-done.42) | copy-start | bytes 3776656
  645.7 14.7 %copy-start.41 = (s32[561,561]{0,1:T(8,128)S(1)}, s32[561,561]{0,1:T(8,128)}, u32[]{:S(2)}) copy-start(s32[561,561]{0,1:T(8,128)} %copy-done.40) | copy-start | bytes 3776656
  660.3 14.9 %copy-start.60 = (f32[768]{0:T(1024)S(1)}, f32[768]{0:T(1024)}, u32[]{:S(2)}) copy-start(f32[768]{0:T(1024)} %get-tuple-element.74) | copy-start | bytes 9220
  660.3 14.9 %copy-start.61 = (f32[768]{0:T(1024)S(1)}, f32[768]{0:T(1024)}, u32[]{:S(2)}) copy-start(f32[768]{0:T(1024)} %get-tuple-element.96) | copy-start | bytes 9220
  660.3 14.9 %copy-start.62 = (f32[768]{0:T(1024)S(1)}, f32[768]{0:T(1024)}, u32[]{:S(2)}) copy-start(f32[768]{0:T(1024)} %get-tuple-element.75) | copy-start | bytes 9220
  660.3 14.9 %copy-start.66 = (f32[768]{0:T(1024)S(1)}, f32[768]{0:T(1024)}, u32[]{:S(2)}) copy-start(f32[768]{0:T(1024)} %get-tuple-element.124) | copy-start | bytes 9220
  813.8 4.1 copy-start.54
  813.8 4.9 copy-start.53
  815.8 3.7 copy-start.25
  819.5 3.9 copy-start.1
  (51 other events, 89.9 us)
Sparse Core Ops, SparseCore 0:
  124.9 77.9 all-reduce.8
  214.4 74.2 all-reduce.10
  303.0 74.2 all-reduce.12
  388.7 74.2 all-reduce.14
  476.3 125.6 all-gather.3
  621.5 73.4 all-reduce.16
  700.8 112.9 all-reduce.18
